TPU v7x, 32 devices: a whole 2x2x4 slice. The times are simulated.
32 devices in a mesh: rows: 8 (over y, x, core), grp: 4 (over z).
Axes of the slice: x: 2, y: 2, z: 4, core: 2. Of those that a mesh axis runs over, the one named last changes fastest.
Arguments:
- date_keys: int32 [262144], P(('rows', 'grp')), may hold values from 0 to 2559
- product_keys: int32 [262144], P(('rows', 'grp')), may hold values from 0 to 16255
- quantity: float32 [262144], P(('rows', 'grp')), may hold values from 0.01 to 10
- date_flags: int32 [2560], P('rows'), may hold values 0 or 1
- category: int32 [16256], P('rows'), may hold values from 0 to 999
- unit_price: float32 [16256], P('rows'), may hold values from 0.5 to 4
- unit_cost: float32 [16256], P('rows'), may hold values from 0.25 to 2
Outputs:
- revenue_by_category: float32 [1000], replicated
- profit_by_category: float32 [1000], replicated
All inputs are finite; a program needn't handle non-finite values. No bound on the sum of `date_flags` on one device may be relied on, other than what follows from the above.
Results may differ from a plain program's by a relative error of at most 0.00005.
Values sent between devices are 32-bit elements; how exact they have to be, the bound alone decides.
A program may use at most 192 MiB of HBM per device.

v0:
```python
import jax
import jax.numpy as jnp
from jax import lax
from jax.sharding import PartitionSpec as P

CATS = 1000


def category_sums(group_ids, amounts):
    length = group_ids.shape[0]
    padded = (CATS + 127) // 128 * 128
    block_rows = min(2048, (length + 127) // 128 * 128)
    total_rows = (length + block_rows - 1) // block_rows * block_rows
    extra = total_rows - length
    group_ids = jnp.concatenate([group_ids, jnp.full((extra,), padded, jnp.int32)])
    amounts = jnp.concatenate([amounts, jnp.zeros((2, extra), jnp.float32)], axis=1)
    columns = lax.broadcasted_iota(jnp.int32, (block_rows, padded), 1)

    def add_block(running, pieces):
        block_ids, block_amounts = pieces
        onehot = (block_ids[:, None] == columns).astype(jnp.float32)
        summed = jnp.dot(
            block_amounts,
            onehot,
            precision=lax.Precision.HIGHEST,
            preferred_element_type=jnp.float32,
        )
        return (running + summed, None)

    stacked = amounts.reshape(2, total_rows // block_rows, block_rows).transpose(1, 0, 2)
    running, _ = lax.scan(
        add_block, jnp.zeros((2, padded), jnp.float32), (group_ids.reshape(-1, block_rows), stacked)
    )
    return running


def window_sums(product_keys, kept_amount, row_count):
    inside = (product_keys >= 0) & (product_keys < row_count)
    segment = jnp.where(inside, product_keys, row_count)
    summed = jax.ops.segment_sum(
        jnp.where(inside, kept_amount, 0.0), segment, num_segments=row_count + 1
    )
    return summed[:row_count]


def body(date_keys, product_keys, quantity, date_flags, category, unit_price, unit_cost):
    date_mask = lax.all_gather(date_flags, "rows", axis=0, tiled=True)
    passed = jnp.take(date_mask, date_keys, axis=0)
    kept_amount = jnp.where(passed == 1, quantity, 0.0)
    shard_len = unit_price.shape[0]
    amount = lax.psum_scatter(
        window_sums(product_keys, kept_amount, shard_len * lax.axis_size("rows")),
        "rows",
        scatter_dimension=0,
        tiled=True,
    )
    revenue = amount * unit_price
    profit = amount * (unit_price - unit_cost)
    partial_value = category_sums(category, jnp.stack([revenue, profit]))
    totals = lax.psum(partial_value, ("rows", "grp"))
    fact_total = date_keys.shape[0] * lax.axis_size("rows") * lax.axis_size("grp")
    factor = CATS / fact_total
    return (totals[0, :CATS] * factor, totals[1, :CATS] * factor)


def solution(mesh):
    return jax.shard_map(
        body,
        mesh=mesh,
        in_specs=(
            P(("rows", "grp")),
            P(("rows", "grp")),
            P(("rows", "grp")),
            P("rows"),
            P("rows"),
            P("rows"),
            P("rows"),
        ),
        out_specs=(P(), P()),
        check_vma=False,
    )
```

profile of v0, /device:TPU:0, one launch (start us, length us, event | category | flops | bytes accessed | tf_op | source)
XLA Modules:
  0.0 184.5 jit_solution(4197366333144670196)
XLA Ops:
  0.6 0.0 copy-start
  0.7 1.3 fusion.16
  2.6 0.9 dynamic-update-slice
  3.5 25.5 %all-reduce.2 = s32[2560]{0:T(1024)S(1)} all-reduce(s32[2560]{0:T(1024)S(1)} %dynamic-update-slice), channel_id=1, replica_groups=mesh['rows'=8,'grp'=4] {'rows'}, use_global_device_ids=true, to_apply=%add.2 | all-reduce | flops 2560 | bytes 20480
  29.1 0.0 copy-done
  29.1 0.0 copy-start.1
  29.1 0.0 copy-start.2
  29.1 45.5 %gather_fusion = s32[8192]{0:T(1024)S(1)} fusion(s32[2560]{0:T(1024)S(1)} %all-reduce.2, s32[8192]{0:T(1024)S(1)} %fusion.4), kind=kCustom, calls=%fused_computation | custom fusion | bytes 98304 | tf_op jit(solution)/shard_map/jit(_take)/gather | solution.py:48
  74.6 0.0 copy-done.1
  74.7 0.0 copy-done.2
  74.7 43.2 %scatter_custom_fusion = f32[16257]{0:T(1024)S(1)} fusion(s32[8192]{0:T(1024)S(1)} %fusion.5, f32[8192]{0:T(1024)S(1)} %select_select_fusion, f32[]{:T(128)} %constant.10.clone.1), kind=kCustom, calls=%fused_computation.8 | custom fusion | flops 8192 | bytes 65032 | tf_op jit(solution)/shard_map/scatter-add | solution.py:40
  117.9 0.0 copy-start.4
  118.0 0.0 copy-start.5
  118.0 0.0 copy-start.3
  118.0 22.9 %all-reduce.3 = f32[16256]{0:T(1024)S(1)} all-reduce(f32[16256]{0:T(1024)S(1)} %bitcast.7), channel_id=2, replica_groups=mesh['rows'=8,'grp'=4] {'rows'}, use_global_device_ids=true, to_apply=%region_1.2.clone | all-reduce | flops 16256 | bytes 130048
  141.5 0.0 copy-done.4
  141.5 0.0 copy-done.5
  141.5 0.1 dynamic-slice_multiply_fusion
  141.6 0.0 copy-done.3
  141.6 2.7 %fusion = f32[2,1024]{1,0:T(2,128)S(1)} fusion(s32[2048]{0:T(1024)S(1)} %concatenate.7, f32[1,2032]{1,0:T(1,128)S(1)} %bitcast.9, f32[1,2032]{1,0:T(1,128)S(1)} %bitcast.8), kind=kOutput, calls=%fused_computation.3 | convolution fusion | flops 52445184 | bytes 32640 | tf_op jit(solution)/shard_map/while/body/eval_jaxpr/dot_general | solution.py:22
  144.4 39.5 %psum.7 = f32[2,1024]{1,0:T(2,128)S(1)} all-reduce(f32[2,1024]{1,0:T(2,128)S(1)} %fusion), channel_id=1, replica_groups=mesh['rows'=8,'grp'=4] {'rows','grp'}, use_global_device_ids=true, to_apply=%region_2.3 | all-reduce | flops 2048 | bytes 16384 | tf_op jit(solution)/shard_map/psum | solution.py:60
  183.9 0.6 slice_multiply_fusion
  (5 shorter events, 0.0 us)
Async XLA Ops:
  0.6 28.4 %copy-start = (s32[8192]{0:T(1024)S(1)}, s32[8192]{0:T(1024)}, u32[]{:S(2)}) copy-start(s32[8192]{0:T(1024)} %param.7) | copy-start | bytes 98308
  29.1 45.6 %copy-start.1 = (s32[8192]{0:T(1024)S(1)}, s32[8192]{0:T(1024)}, u32[]{:S(2)}) copy-start(s32[8192]{0:T(1024)} %param.8) | copy-start | bytes 98308
  29.1 45.6 %copy-start.2 = (f32[8192]{0:T(1024)S(1)}, f32[8192]{0:T(1024)}, u32[]{:S(2)}) copy-start(f32[8192]{0:T(1024)} %param.9) | copy-start | bytes 98308
  117.9 23.6 %copy-start.4 = (f32[2032]{0:T(1024)S(1)}, f32[2032]{0:T(1024)}, u32[]{:S(2)}) copy-start(f32[2032]{0:T(1024)} %param.12) | copy-start | bytes 24388
  118.0 23.6 %copy-start.5 = (f32[2032]{0:T(1024)S(1)}, f32[2032]{0:T(1024)}, u32[]{:S(2)}) copy-start(f32[2032]{0:T(1024)} %param.13) | copy-start | bytes 24388
  118.0 23.6 %copy-start.3 = (s32[2032]{0:T(1024)S(1)}, s32[2032]{0:T(1024)}, u32[]{:S(2)}) copy-start(s32[2032]{0:T(1024)} %param.11) | copy-start | bytes 24388
where the time goes:
time: 185 us
  blocking collectives  87.9 us (48%)
  local copies, waits for them, and re-layouts  47.8 us (26%)
  other arithmetic  44 us (24%)
  matrix products  2.74 us (1%)
  between operations  2.08 us (1%)
    unnamed x2, blocking collectives  48.4 us
    gather x1, local copies, waits for them, and re-layouts, body(): passed = jnp.take(date_mask, date_keys, axis=0)  45.5 us
    scatter-add x1, other arithmetic, window_sums(): jax.ops.segment_sum(jnp.where(inside, kept_amount, 0.0), segment, num_seg...  43.2 us
    psum x1, blocking collectives, body(): totals = lax.psum(partial_value, ('rows', 'grp'))  39.5 us

commit v1 on v0

--- a/solution.py
+++ b/solution.py
@@ -4,6 +4,11 @@
 from jax.sharding import PartitionSpec as P
 
 CATS = 1000
+
+
+def add_all(x, mesh_axis):
+    parts = lax.all_gather(x, mesh_axis)
+    return jnp.sum(parts, axis=0)
 
 
 def category_sums(group_ids, amounts):
@@ -57,7 +62,7 @@
     revenue = amount * unit_price
     profit = amount * (unit_price - unit_cost)
     partial_value = category_sums(category, jnp.stack([revenue, profit]))
-    totals = lax.psum(partial_value, ("rows", "grp"))
+    totals = add_all(partial_value, ("rows", "grp"))
     fact_total = date_keys.shape[0] * lax.axis_size("rows") * lax.axis_size("grp")
     factor = CATS / fact_total
     return (totals[0, :CATS] * factor, totals[1, :CATS] * factor)

time: 185 us -> 215 us (1.16)
  blocking collectives: 87.9 us -> 117 us
    all_gather x0 -> x1, blocking collectives: none -> 68.6 us  [add_all(): parts = lax.all_gather(x, mesh_axis)]
    psum x1 -> x0, blocking collectives: 39.5 us -> none  [body(): totals = lax.psum(partial_value, ('rows', 'grp'))]
where the time goes in v1:
time: 215 us
  blocking collectives  117 us (54%)
  local copies, waits for them, and re-layouts  48.5 us (23%)
  other arithmetic  44.8 us (21%)
  matrix products  2.74 us (1%)
    all_gather x1, blocking collectives, add_all(): parts = lax.all_gather(x, mesh_axis)  68.6 us
    unnamed x2, blocking collectives  48.3 us
    gather x1, local copies, waits for them, and re-layouts, body(): passed = jnp.take(date_mask, date_keys, axis=0)  45.5 us
    scatter-add x1, other arithmetic, window_sums(): jax.ops.segment_sum(jnp.where(inside, kept_amount, 0.0), segment, num_seg...  43.2 us

profile of v1, /device:TPU:0, one launch (start us, length us, event | category | flops | bytes accessed | tf_op | source)
XLA Modules:
  0.0 214.9 jit_solution(8552686019833655639)
XLA Ops:
  0.6 1.3 fusion.17
  3.3 0.7 concatenate.7
  4.0 0.9 dynamic-update-slice
  4.8 25.5 %all-reduce.2 = s32[2560]{0:T(1024)S(1)} all-reduce(s32[2560]{0:T(1024)S(1)} %dynamic-update-slice), channel_id=1, replica_groups=mesh['rows'=8,'grp'=4] {'rows'}, use_global_device_ids=true, to_apply=%add.2 | all-reduce | flops 2560 | bytes 20480
  30.4 0.8 fusion.5
  31.1 0.0 copy-start
  31.1 0.0 copy-start.1
  31.1 0.0 copy-start.2
  31.2 45.5 %gather_fusion = s32[8192]{0:T(1024)S(1)} fusion(s32[2560]{0:T(1024)S(1)} %all-reduce.2, s32[8192]{0:T(1024)S(1)} %fusion.5), kind=kCustom, calls=%fused_computation | custom fusion | bytes 98304 | tf_op jit(solution)/shard_map/jit(_take)/gather | solution.py:53
  76.7 0.0 copy-done
  76.7 0.0 copy-done.1
  76.7 0.0 copy-done.2
  76.7 0.0 copy-start.3
  76.7 0.0 copy-start.4
  76.8 43.2 %scatter_custom_fusion = f32[16257]{0:T(1024)S(1)} fusion(s32[8192]{0:T(1024)S(1)} %fusion.6, f32[8192]{0:T(1024)S(1)} %select_select_fusion, f32[]{:T(128)} %constant.10.clone.1), kind=kCustom, calls=%fused_computation.9 | custom fusion | flops 8192 | bytes 65032 | tf_op jit(solution)/shard_map/scatter-add | solution.py:45
  120.0 22.7 %all-reduce.3 = f32[16256]{0:T(1024)S(1)} all-reduce(f32[16256]{0:T(1024)S(1)} %bitcast.9), channel_id=3, replica_groups=mesh['rows'=8,'grp'=4] {'rows'}, use_global_device_ids=true, to_apply=%region_1.2.clone | all-reduce | flops 16256 | bytes 130048
  142.8 0.0 copy-done.3
  142.8 0.0 copy-done.4
  142.8 0.1 dynamic-slice_multiply_fusion
  142.9 2.7 %fusion.2 = f32[1,2,1024]{2,1,0:T(2,128)S(1)} fusion(s32[2048]{0:T(1024)S(1)} %concatenate.7, f32[1,2032]{1,0:T(1,128)S(1)} %bitcast.11, f32[1,2032]{1,0:T(1,128)S(1)} %bitcast.10), kind=kOutput, calls=%fused_computation.5 | convolution fusion | flops 52445184 | bytes 32640 | tf_op jit(solution)/shard_map/while/body/eval_jaxpr/dot_general | solution.py:27
  145.6 68.6 %all-gather.1 = f32[32,2,1024]{2,1,0:T(2,128)S(1)} all-gather(f32[1,2,1024]{2,1,0:T(2,128)S(1)} %fusion.2), channel_id=2, replica_groups=mesh['rows'=8,'grp'=4] {'rows','grp'}, dimensions={0}, use_global_device_ids=true | all-gather | bytes 270336 | tf_op jit(solution)/shard_map/all_gather | solution.py:10
  214.2 0.1 reduce_sum.9
  214.3 0.6 slice_multiply_fusion
  (3 shorter events, 0.0 us)
Async XLA Ops:
  31.1 45.6 %copy-start = (s32[8192]{0:T(1024)S(1)}, s32[8192]{0:T(1024)}, u32[]{:S(2)}) copy-start(s32[8192]{0:T(1024)} %param.7) | copy-start | bytes 98308
  31.1 45.6 %copy-start.1 = (s32[8192]{0:T(1024)S(1)}, s32[8192]{0:T(1024)}, u32[]{:S(2)}) copy-start(s32[8192]{0:T(1024)} %param.8) | copy-start | bytes 98308
  31.1 45.6 %copy-start.2 = (f32[8192]{0:T(1024)S(1)}, f32[8192]{0:T(1024)}, u32[]{:S(2)}) copy-start(f32[8192]{0:T(1024)} %param.9) | copy-start | bytes 98308
  76.7 66.0 %copy-start.3 = (f32[2032]{0:T(1024)S(1)}, f32[2032]{0:T(1024)}, u32[]{:S(2)}) copy-start(f32[2032]{0:T(1024)} %param.12) | copy-start | bytes 24388
  76.7 66.0 %copy-start.4 = (f32[2032]{0:T(1024)S(1)}, f32[2032]{0:T(1024)}, u32[]{:S(2)}) copy-start(f32[2032]{0:T(1024)} %param.13) | copy-start | bytes 24388

commit v2 on v0

--- a/solution.py
+++ b/solution.py
@@ -2,6 +2,7 @@
 import jax.numpy as jnp
 from jax import lax
 from jax.sharding import PartitionSpec as P
+from jax.lax import psum
 
 CATS = 1000
 
@@ -57,7 +58,7 @@
     revenue = amount * unit_price
     profit = amount * (unit_price - unit_cost)
     partial_value = category_sums(category, jnp.stack([revenue, profit]))
-    totals = lax.psum(partial_value, ("rows", "grp"))
+    totals = psum(psum(partial_value, "grp"), "rows")
     fact_total = date_keys.shape[0] * lax.axis_size("rows") * lax.axis_size("grp")
     factor = CATS / fact_total
     return (totals[0, :CATS] * factor, totals[1, :CATS] * factor)

time: 185 us -> 170 us (0.919)
  blocking collectives: 87.9 us -> 72.6 us
    psum x1 -> x2, blocking collectives: 39.5 us -> 24.2 us  [body(): totals = psum(psum(partial_value, 'grp'), 'rows')]
where the time goes in v2:
time: 170 us; the launch traced here: 169 us
  blocking collectives  72.6 us (43%)
  local copies, waits for them, and re-layouts  47.8 us (28%)
  other arithmetic  44 us (26%)
  matrix products  2.74 us (2%)
  between operations  2.09 us (1%)
    unnamed x2, blocking collectives  48.4 us
    gather x1, local copies, waits for them, and re-layouts, body(): passed = jnp.take(date_mask, date_keys, axis=0)  45.5 us
    scatter-add x1, other arithmetic, window_sums(): jax.ops.segment_sum(jnp.where(inside, kept_amount, 0.0), segment, num_seg...  43.2 us
    psum x2, blocking collectives, body(): totals = psum(psum(partial_value, 'grp'), 'rows')  24.2 us

profile of v2, /device:TPU:0, one launch (start us, length us, event | category | flops | bytes accessed | tf_op | source)
XLA Modules:
  0.0 169.2 jit_solution(14713599832865144725)
XLA Ops:
  0.6 0.0 copy-start
  0.7 1.3 fusion.16
  2.6 0.9 dynamic-update-slice
  3.5 25.5 %all-reduce.2 = s32[2560]{0:T(1024)S(1)} all-reduce(s32[2560]{0:T(1024)S(1)} %dynamic-update-slice), channel_id=1, replica_groups=mesh['rows'=8,'grp'=4] {'rows'}, use_global_device_ids=true, to_apply=%add.2 | all-reduce | flops 2560 | bytes 20480
  29.1 0.0 copy-done
  29.1 0.0 copy-start.1
  29.1 0.0 copy-start.2
  29.1 45.5 %gather_fusion = s32[8192]{0:T(1024)S(1)} fusion(s32[2560]{0:T(1024)S(1)} %all-reduce.2, s32[8192]{0:T(1024)S(1)} %fusion.4), kind=kCustom, calls=%fused_computation | custom fusion | bytes 98304 | tf_op jit(solution)/shard_map/jit(_take)/gather | solution.py:49
  74.6 0.0 copy-done.1
  74.7 0.0 copy-done.2
  74.7 43.2 %scatter_custom_fusion = f32[16257]{0:T(1024)S(1)} fusion(s32[8192]{0:T(1024)S(1)} %fusion.5, f32[8192]{0:T(1024)S(1)} %select_select_fusion, f32[]{:T(128)} %constant.10.clone.1), kind=kCustom, calls=%fused_computation.8 | custom fusion | flops 8192 | bytes 65032 | tf_op jit(solution)/shard_map/scatter-add | solution.py:41
  117.9 0.0 copy-start.4
  118.0 0.0 copy-start.5
  118.0 0.0 copy-start.3
  118.0 22.9 %all-reduce.3 = f32[16256]{0:T(1024)S(1)} all-reduce(f32[16256]{0:T(1024)S(1)} %bitcast.7), channel_id=2, replica_groups=mesh['rows'=8,'grp'=4] {'rows'}, use_global_device_ids=true, to_apply=%region_1.2.clone | all-reduce | flops 16256 | bytes 130048
  141.5 0.0 copy-done.4
  141.5 0.0 copy-done.5
  141.5 0.1 dynamic-slice_multiply_fusion
  141.6 0.0 copy-done.3
  141.6 2.7 %fusion = f32[2,1024]{1,0:T(2,128)S(1)} fusion(s32[2048]{0:T(1024)S(1)} %concatenate.7, f32[1,2032]{1,0:T(1,128)S(1)} %bitcast.9, f32[1,2032]{1,0:T(1,128)S(1)} %bitcast.8), kind=kOutput, calls=%fused_computation.3 | convolution fusion | flops 52445184 | bytes 32640 | tf_op jit(solution)/shard_map/while/body/eval_jaxpr/dot_general | solution.py:23
  144.4 12.1 %psum.14 = f32[2,1024]{1,0:T(2,128)S(1)} all-reduce(f32[2,1024]{1,0:T(2,128)S(1)} %fusion), channel_id=1, replica_groups=mesh['rows'=8,'grp'=4] {'grp'}, use_global_device_ids=true, to_apply=%region_2.3 | all-reduce | flops 2048 | bytes 16384 | tf_op jit(solution)/shard_map/psum | solution.py:61
  156.5 12.1 %psum.15 = f32[2,1024]{1,0:T(2,128)S(1)} all-reduce(f32[2,1024]{1,0:T(2,128)S(1)} %psum.14), channel_id=1, replica_groups=mesh['rows'=8,'grp'=4] {'rows'}, use_global_device_ids=true, to_apply=%region_3.4 | all-reduce | flops 2048 | bytes 16384 | tf_op jit(solution)/shard_map/psum | solution.py:61
  168.6 0.6 slice_multiply_fusion
  (5 shorter events, 0.0 us)
Async XLA Ops:
  0.6 28.4 %copy-start = (s32[8192]{0:T(1024)S(1)}, s32[8192]{0:T(1024)}, u32[]{:S(2)}) copy-start(s32[8192]{0:T(1024)} %param.7) | copy-start | bytes 98308
  29.1 45.6 %copy-start.1 = (s32[8192]{0:T(1024)S(1)}, s32[8192]{0:T(1024)}, u32[]{:S(2)}) copy-start(s32[8192]{0:T(1024)} %param.8) | copy-start | bytes 98308
  29.1 45.6 %copy-start.2 = (f32[8192]{0:T(1024)S(1)}, f32[8192]{0:T(1024)}, u32[]{:S(2)}) copy-start(f32[8192]{0:T(1024)} %param.9) | copy-start | bytes 98308
  117.9 23.6 %copy-start.4 = (f32[2032]{0:T(1024)S(1)}, f32[2032]{0:T(1024)}, u32[]{:S(2)}) copy-start(f32[2032]{0:T(1024)} %param.12) | copy-start | bytes 24388
  118.0 23.6 %copy-start.5 = (f32[2032]{0:T(1024)S(1)}, f32[2032]{0:T(1024)}, u32[]{:S(2)}) copy-start(f32[2032]{0:T(1024)} %param.13) | copy-start | bytes 24388
  118.0 23.6 %copy-start.3 = (s32[2032]{0:T(1024)S(1)}, s32[2032]{0:T(1024)}, u32[]{:S(2)}) copy-start(s32[2032]{0:T(1024)} %param.11) | copy-start | bytes 24388
